TPU v7x, 256 devices: a whole 4x4x8 slice. The times are simulated.
256 devices in a mesh: row: 32 (over z_hi, y, core), col: 8 (over z_lo, x).
Axes of the slice: x: 4, y: 4, z: 8 (z_hi: 4, z_lo: 2; z = z_hi * 2 + z_lo), core: 2. Of those that a mesh axis runs over, the one named last changes fastest.
Arguments:
- matrix: float32 [16384, 16384], P('row', 'col'), as said below
- inverse_blocks: float32 [2, 256, 256], replicated, as said below
- pivots: int32 [512], replicated, may hold values from 0 to 16383, as said below
Outputs:
- updated: float32 [16384, 16384], P('row', 'col')
- factor: float32 [16384, 512], P('row')
Inputs may be any that keep to these rules, and one draw needn't show every extreme that they name: matrix is exactly symmetric. `inverse_blocks`: each block is exactly symmetric. pivots[i] is i or at least 512; the entries of at least 512 are distinct; pivots[0] is 0; the last entry is 16383.
All inputs are finite; a program needn't handle non-finite values.
Results may differ from a plain program's by a relative error of at most 0.00018.
Values sent between devices are 32-bit elements; how exact they have to be, the bound alone decides.
A program may use at most 64 MiB of HBM per device.

v0:
```python
import jax
import jax.numpy as jnp
from jax import lax
from jax.sharding import PartitionSpec as P


def product(left, right):
    return jnp.dot(left, right, precision=lax.Precision.HIGHEST, preferred_element_type=jnp.float32)


def outside(indices, chosen):
    return 1.0 - jnp.any(indices[:, None] == chosen[None, :], axis=1).astype(jnp.float32)


def select_columns(source, wanted, col_start):
    local_idx = wanted - col_start
    inside = (local_idx >= 0) & (local_idx < source.shape[1])
    picked_cols = jnp.take(source, jnp.clip(local_idx, 0, source.shape[1] - 1), axis=1)
    return jnp.where(inside[None, :], picked_cols, 0.0)


def select_rows(source, wanted, row_start):
    local_idx = wanted - row_start
    inside = (local_idx >= 0) & (local_idx < source.shape[0])
    picked_rows = jnp.take(source, jnp.clip(local_idx, 0, source.shape[0] - 1), axis=0)
    return jnp.where(inside[:, None], picked_rows, 0.0)


def shards(matrix, inverse_blocks, pivots):
    tile_rows, tile_cols = matrix.shape
    width = inverse_blocks.shape[1]
    row_start = lax.axis_index("row") * tile_rows
    col_start = lax.axis_index("col") * tile_cols
    row_ids = row_start + jnp.arange(tile_rows, dtype=jnp.int32)
    col_ids = col_start + jnp.arange(tile_cols, dtype=jnp.int32)
    first_pivots = pivots[:width]
    second_pivots = pivots[width:]
    row_panel = lax.psum(select_columns(matrix, pivots, col_start), "col")
    ratio = lax.axis_size("row") // lax.axis_size("col")
    owner = lax.axis_index("row") // ratio
    place = lax.axis_index("row") % ratio
    slots = jnp.zeros((pivots.shape[0], ratio, tile_rows), jnp.float32)
    slots = lax.dynamic_update_slice(
        slots, row_panel.T[:, None, :], (jnp.int32(0), place, jnp.int32(0))
    )
    slots = jnp.where(owner == lax.axis_index("col"), slots, 0.0)
    across = lax.psum(slots, "row").reshape(pivots.shape[0], tile_cols)
    weights_one = inverse_blocks[0]
    weights_two = inverse_blocks[1]
    live_rows_one = outside(row_ids, first_pivots)
    live_cols_one = outside(col_ids, first_pivots)
    live_rows_two = outside(row_ids, pivots)
    live_cols_two = outside(col_ids, pivots)
    panel_rows_one = row_panel[:, :width]
    factor_rows_one = product(panel_rows_one, weights_one)
    factor_cols_one = product(weights_one.T, across[:width])
    shrunk = matrix - live_rows_one[:, None] * live_cols_one[None, :] * product(
        factor_rows_one, across[:width]
    )
    local_block = select_columns(
        select_rows(matrix, second_pivots, row_start), first_pivots, col_start
    )
    corner = lax.psum(local_block, ("row", "col"))
    panel_rows_two = row_panel[:, width:] - live_rows_one[:, None] * product(
        factor_rows_one, corner.T
    )
    panel_cols_two = across[width:] - live_cols_one[None, :] * product(corner, factor_cols_one)
    factor_rows_two = product(panel_rows_two, weights_two)
    updated = shrunk - live_rows_two[:, None] * live_cols_two[None, :] * product(
        factor_rows_two, panel_cols_two
    )
    factor = jnp.concatenate(
        [live_rows_one[:, None] * factor_rows_one, live_rows_two[:, None] * factor_rows_two], axis=1
    )
    return (updated, factor)


def solution(mesh):
    return jax.shard_map(
        shards,
        mesh=mesh,
        in_specs=(P("row", "col"), P(), P()),
        out_specs=(P("row", "col"), P("row", None)),
        check_vma=False,
    )
```

profile of v0, /device:TPU:1, one launch (start us, length us, event | category | flops | bytes accessed | tf_op | source)
XLA Modules:
  0.0 706.8 jit_solution(16723641824497949463)
XLA Ops:
  7.2 0.0 all-reduce.4.cloned.1.call-start
  7.2 0.7 compare_and_fusion.4
  7.9 5.3 copy.16
  13.3 4.2 gather_fusion
  17.5 0.3 copy.17
  17.8 0.1 select_bitcast_fusion
  18.0 0.0 copy-start.5
  18.0 1.3 copy.18
  19.3 0.0 all-reduce.4.cloned.1.call-update
  19.3 0.0 all-reduce.8.cloned.1.call-start
  19.4 0.0 copy-done.5
  19.4 4.6 gather_fusion.1
  24.0 1.6 select_select_fusion
  25.6 1.9 copy.20
  27.5 1.0 gather_fusion.2
  28.5 0.8 select_bitcast_fusion.2
  29.4 0.0 all-reduce.8.cloned.1.call-update
  29.4 0.2 all-reduce.6.cloned.1.call-start
  29.6 70.8 %all-reduce.4.cloned.1.call-done = f32[512,512]{0,1:T(8,128)} async-done(((f32[512,512]{0,1:T(8,128)}), f32[512,512]{0,1:T(8,128)}) %all-reduce.4.cloned.1.call-update) | async-done | bytes 1048592 | tf_op jit(solution)/shard_map/psum | solution.py:38
  100.4 1.3 select_bitcast_fusion.1
  101.7 0.3 copy.19
  102.1 2.5 broadcast_in_dim.102
  104.6 1.0 constant_dynamic-update-slice_fusion
  105.6 0.0 copy-start.1
  105.6 0.0 copy-start.2
  105.7 0.0 all-reduce.6.cloned.1.call-update
  105.7 0.2 compare_reduce_fusion.3
  105.9 0.3 compare_reduce_fusion.2
  106.2 0.6 compare_reduce_fusion.1
  106.8 0.9 compare_reduce_fusion
  107.7 0.0 copy-done.1
  107.8 0.0 copy-done.2
  107.8 0.7 broadcast_multiply_fusion.1
  108.4 255.0 %all-reduce.8.cloned.1.call-done = f32[256,256]{0,1:T(8,128)} async-done(((f32[256,256]{0,1:T(8,128)}), f32[256,256]{0,1:T(8,128)}) %all-reduce.8.cloned.1.call-update) | async-done | bytes 262160 | tf_op jit(solution)/shard_map/psum | solution.py:63
  363.5 1.6 fusion.1
  365.1 1.6 broadcast_multiply_fusion
  366.7 0.1 pad_maximum_fusion
  366.8 1.3 copy.23
  368.1 302.4 %all-reduce.6.cloned.1.call-done = f32[512,4,512]{0,2,1:T(8,128)} async-done(((f32[512,4,512]{0,2,1:T(8,128)}), f32[512,4,512]{0,2,1:T(8,128)}) %all-reduce.6.cloned.1.call-update) | async-done | bytes 4194320 | tf_op jit(solution)/shard_map/psum | solution.py:47
  670.5 4.0 fusion.12
  674.5 0.0 copy-done.3
  674.5 1.8 fusion.6
  676.3 8.3 %fusion.13 = f32[512,2048]{1,0:T(8,128)} fusion(f32[512,256]{0,1:T(8,128)S(1)} %get-tuple-element.26, f32[256,2048]{0,1:T(8,128)S(1)} %bitcast.33), kind=kOutput, calls=%fused_computation.50 | convolution fusion | flops 3221225472 | bytes 6815744 | tf_op jit(solution)/shard_map/dot_general | solution.py:8
  684.6 3.0 copy.22
  687.6 0.0 copy-done.4
  687.6 5.2 fusion
  692.8 0.0 copy-done
  692.8 7.5 %multiply_subtract_fusion = f32[512,2048]{1,0:T(8,128)} fusion(f32[512,2048]{1,0:T(8,128)S(1)} %copy-done, f32[512,2048]{1,0:T(8,128)} %fusion.13, f32[512,256]{0,1:T(8,128)S(1)} %get-tuple-element.24, f32[256,2048]{1,0:T(8,128)S(1)} %fusion, f32[2048]{0:T(1024)S(1)} %get-tuple-element.29, f32[512]{0:T(512)S(1)} %get-tuple-element.31, ...), kind=kOutput, calls=%fused_computation.3 | convolution fusion | flops 3227516928 | bytes 15224832 | tf_op jit(solution)/shard_map/dot_general | solution.py:8
  (11 shorter events, 0.1 us)
Async XLA Ops:
  7.2 93.2 %all-reduce.4.cloned.1.call-start = ((), (), s32[]{:S(2)}) async-start(), calls=%async_computation | async-start | bytes 2097152 | tf_op jit(solution)/shard_map/psum | solution.py:38
  18.0 1.4 copy-start.5
  19.3 344.2 %all-reduce.8.cloned.1.call-start = ((), (), s32[]{:S(2)}) async-start(), calls=%async_computation.2 | async-start | bytes 524288 | tf_op jit(solution)/shard_map/psum | solution.py:63
  29.4 641.1 %all-reduce.6.cloned.1.call-start = ((), (), s32[]{:S(2)}) async-start(), calls=%async_computation.1 | async-start | bytes 8388608 | tf_op jit(solution)/shard_map/psum | solution.py:47
  105.6 2.1 copy-start.1
  105.6 2.1 copy-start.2
  670.5 4.0 copy-start.3
  684.6 3.0 copy-start.4
  687.6 5.2 copy-start
Sparse Core Ops, SparseCore 0:
  19.4 80.9 all-reduce.3
  105.9 257.5 all-reduce.7
  366.7 303.7 all-reduce.5
where the time goes:
time: 707 us
  waiting for transfers between devices  628 us (89%)
  local copies, waits for them, and re-layouts  30.9 us (4%)
  matrix products  26.7 us (4%)
  between operations  14 us (2%)
    psum x1, waiting for transfers between devices, shards(): across = lax.psum(slots, 'row').reshape(pivots.shape[0], tile_cols)  302 us
    psum x1, waiting for transfers between devices, shards(): corner = lax.psum(local_block, ('row', 'col'))  255 us
    psum x1, waiting for transfers between devices, shards(): row_panel = lax.psum(select_columns(matrix, pivots, col_start), 'col')  70.8 us
    dot_general x7, matrix products, product(): jnp.dot(left, right, precision=lax.Precision.HIGHEST, preferred_element_t...  26.7 us
  transfers between devices with their start and end apart: 3, of which 3 were waited for; matrix products, arithmetic and copies ran while one was open for 3% of the time, Pallas kernels for 0%

commit v1 on v0

v1 whole, which is shorter than its diff:
```python
import jax
import jax.numpy as jnp
from jax import lax
from jax.experimental import pallas as pl
from jax.experimental.pallas import tpu as pltpu
from jax.sharding import PartitionSpec as P

MESH = pl.DeviceIdType.MESH
F32, BF16 = jnp.float32, jnp.bfloat16
ROWS, COLS, NB, NP = 512, 2048, 256, 512
PARTS, LANES = 4, 128
PIECE, EXTRA = 64, 16
SLICE = PIECE + EXTRA
ORDERS = (("xa", "xb", "zl"), ("xb", "xa", "zl"), ("zl", "xa", "xb"), ("zl", "xb", "xa"))
Z_ORDERS = (("za", "zb"), ("zb", "za"), ("za", "zb"), ("zb", "za"))
Y_ORDERS = (("ya", "yb"), ("yb", "ya"), ("yb", "ya"), ("ya", "yb"))
CORNER_ORDER = ("xa", "xb", "zl")
CORNER_SUM = ("co", "ya", "yb", "za", "zb")


def flip_a(v):
    return v + 1 - 2 * (v % 2)


def flip_b(v):
    return (v + 2 * (v % 2) + 3) % 4


def bit_a(v):
    return ((v + 1) // 2) % 2


def bit_b(v):
    return v // 2


def target_bits(s):
    x, zl = s % 4, s // 4
    return {"xa": bit_a(x), "xb": bit_b(x), "zl": zl}


def slot_of(order, s):
    b = target_bits(s)
    return b[order[0]] * 4 + b[order[1]] * 2 + b[order[2]]


def split(a):
    hi = a.astype(BF16)
    return hi, (a - hi.astype(F32)).astype(BF16)


def dot(a, b, dims):
    return lax.dot_general(a, b, (dims, ((), ())), preferred_element_type=F32)


def dot3(a, b, dims):
    (ah, al), (bh, bl) = a, b
    return dot(ah, bh, dims) + (dot(ah, bl, dims) + dot(al, bh, dims))


NN = ((1,), (0,))
NT = ((1,), (1,))
TN = ((0,), (0,))


def select_kernel(pivots_ref, m_ref, out_ref, acc):
    k = pl.program_id(0)
    row_start = lax.axis_index("row") * ROWS
    width = m_ref.shape[1]
    col_start = lax.axis_index("col") * COLS + k * width
    pivots = pivots_ref[...]
    ids = lax.broadcasted_iota(jnp.int32, (width, NP), 0) + col_start
    onehot = (ids == pivots).astype(F32).astype(BF16)
    hi, lo = split(m_ref[...])
    part = dot(hi, onehot, NN) + dot(lo, onehot, NN)

    @pl.when(k == 0)
    def _():
        acc[...] = part

    @pl.when(k > 0)
    def _():
        acc[...] += part

    @pl.when(k == pl.num_programs(0) - 1)
    def _():
        rows = lax.broadcasted_iota(jnp.int32, (ROWS, NB), 0) + row_start
        chosen = (rows == pivots[:, NB:]).astype(F32).astype(BF16)
        hi, lo = split(acc[:, :NB])
        corner = dot(chosen, hi, TN) + dot(chosen, lo, TN)
        for p in range(PARTS):
            for s in range(8):
                at = slot_of(ORDERS[p], s) * SLICE
                out_ref[p, at : at + PIECE, :] = acc[
                    s * PIECE : (s + 1) * PIECE, p * LANES : (p + 1) * LANES
                ]
                first = (p // 2) * 128 + s * EXTRA
                lane = (p % 2) * LANES
                out_ref[p, at + PIECE : at + SLICE, :] = corner[
                    first : first + EXTRA, lane : lane + LANES
                ]


def exchange_kernel(
    s_ref, c_ref, r_ref, k_ref, rx, sum_one, sum_two, q, ar, arx, send_sem, recv_sem, own_sem
):
    row, col = lax.axis_index("row"), lax.axis_index("col")
    zh, y, core = row // 8, (row % 8) // 2, row % 2
    zl, x = col // 4, col % 4
    bits = {"xa": bit_a(x), "xb": bit_b(x), "zl": zl}

    def device(zh_, y_, core_, zl_, x_):
        return (zh_ * 8 + y_ * 2 + core_, zl_ * 4 + x_)

    def storage(zh_, y_, core_):
        return y_ * 8 + core_ * 4 + zh_

    partner = {
        "xa": device(zh, y, core, zl, flip_a(x)),
        "xb": device(zh, y, core, zl, flip_b(x)),
        "zl": device(zh, y, core, 1 - zl, x),
        "za": device(flip_a(zh), y, core, zl, x),
        "zb": device(flip_b(zh), y, core, zl, x),
        "ya": device(zh, flip_a(y), core, zl, x),
        "yb": device(zh, flip_b(y), core, zl, x),
        "co": device(zh, y, 1 - core, zl, x),
    }
    flipped = {
        "za": flip_a(zh),
        "zb": flip_b(zh),
        "ya": flip_a(y),
        "yb": flip_b(y),
        "zz": (zh + 2) % 4,
        "yy": (y + 2) % 4,
    }
    dest = device(zl * 2 + x % 2, (y % 2) * 2 + x // 2, core, zh // 2, (zh % 2) * 2 + y // 2)
    dest_slot = storage(zl * 2 + x % 2, (y % 2) * 2 + x // 2, core)
    source = device(zl * 2 + x // 2, (x % 2) * 2 + y // 2, core, zh // 2, (y % 2) * 2 + zh % 2)
    is_self = (dest[0] == row) & (dest[1] == col)
    not_self = jnp.logical_not(is_self)

    barrier = pltpu.get_barrier_semaphore()

    def greet(dev):
        pl.semaphore_signal(barrier, inc=1, device_id=dev, device_id_type=MESH)

    for dev in partner.values():
        greet(dev)

    @pl.when(not_self)
    def _():
        greet(dest)
        greet(source)
        pl.semaphore_wait(barrier, len(partner) + 2)

    @pl.when(is_self)
    def _():
        pl.semaphore_wait(barrier, len(partner))

    ids = {}
    sent = []

    def copy(key, src, dst, dev):
        n = ids.setdefault(key, len(ids))
        return pltpu.make_async_remote_copy(
            src_ref=src,
            dst_ref=dst,
            send_sem=send_sem.at[n],
            recv_sem=recv_sem.at[n],
            device_id=dev,
            device_id_type=MESH,
        )

    def send(key, src, dst, dim):
        c = copy(key, src, dst, partner[dim])
        c.start()
        sent.append(c)

    def arrive(key, dst, dim):
        copy(key, dst, dst, partner[dim]).wait_recv()

    def at(ref, p, start, size):
        return ref.at[p, pl.ds(pl.multiple_of(start, 8), size), :]

    def load(ref, p, start, size):
        return ref[p, pl.ds(pl.multiple_of(start, 8), size), :]

    R1, R2, R3 = 4 * SLICE, 2 * SLICE, SLICE

    def rx_at(p, n):
        return rx.at[p, (0, R1, R1 + R2)[n] : (R1, R1 + R2, R1 + R2 + R3)[n], :]

    for p in range(PARTS):
        d = ORDERS[p][0]
        send(("rs0", p), at(s_ref, p, (1 - bits[d]) * R1, R1), rx_at(p, 0), d)
    for p in range(PARTS):
        d, e = ORDERS[p][:2]
        arrive(("rs0", p), rx_at(p, 0), d)
        sum_one[p] = load(s_ref, p, bits[d] * R1, R1) + rx[p, :R1, :]
        send(("rs1", p), at(sum_one, p, (1 - bits[e]) * R2, R2), rx_at(p, 1), e)
    for p in range(PARTS):
        d, e = ORDERS[p][1:]
        arrive(("rs1", p), rx_at(p, 1), d)
        sum_two[p] = load(sum_one, p, bits[d] * R2, R2) + rx[p, R1 : R1 + R2, :]
        send(("rs2", p), at(sum_two, p, (1 - bits[e]) * R3, R3), rx_at(p, 2), e)

    mine = storage(zh, y, core)

    def c_at(p, slot, count):
        return at(c_ref, p, slot * PIECE, count * PIECE)

    def place(p):
        return copy(("place", p), q.at[p, :PIECE, :], c_at(p, dest_slot, 1), dest)

    def keep(p):
        return pltpu.make_async_copy(q.at[p, :PIECE, :], c_at(p, dest_slot, 1), own_sem.at[p])

    def r_slot(p):
        a, b, c = ORDERS[p]
        return bits[a] * 4 + bits[b] * 2 + bits[c]

    def r_at(p, slot, count):
        return at(r_ref, p, slot * PIECE, count * PIECE)

    for p in range(PARTS):
        d = ORDERS[p][2]
        arrive(("rs2", p), rx_at(p, 2), d)
        q[p] = load(sum_two, p, bits[d] * R3, R3) + rx[p, R1 + R2 :, :]

        @pl.when(not_self)
        def _(p=p):
            place(p).start()

        @pl.when(is_self)
        def _(p=p):
            keep(p).start()

        r_ref[p, pl.ds(pl.multiple_of(r_slot(p) * PIECE, 8), PIECE), :] = q[p, :PIECE, :]
        send(("r0", p), q.at[p, :PIECE, :], r_at(p, r_slot(p), 1), d)
        ar[0, p * EXTRA : (p + 1) * EXTRA, :] = q[p, PIECE:, :]

    def corner_send(n):
        send(("ar", n), ar.at[n], arx.at[n], CORNER_SUM[n])

    def corner_add(n):
        arrive(("ar", n), arx.at[n], CORNER_SUM[n])
        ar[n + 1] = ar[n] + arx[n]

    corner_send(0)

    for p in range(PARTS):

        @pl.when(not_self)
        def _(p=p):
            copy(("place", p), c_at(p, mine, 1), c_at(p, mine, 1), source).wait_recv()

        @pl.when(is_self)
        def _(p=p):
            keep(p).wait()

        z0, z1 = Z_ORDERS[p]
        send(("z0", p), c_at(p, mine, 1), c_at(p, mine, 1), z0)
        send(("z1", p), c_at(p, mine, 1), c_at(p, mine, 1), z1)
        if p == 0:
            corner_add(0)
            corner_send(1)

    for p in range(PARTS):
        z0, z1 = Z_ORDERS[p]
        near = storage(flipped[z0], y, core)
        arrive(("z0", p), c_at(p, near, 1), z0)
        send(("z2", p), c_at(p, near, 1), c_at(p, near, 1), z1)
    corner_add(1)
    corner_send(2)

    group = storage(0, y, core)
    for p in range(PARTS):
        z0, z1 = Z_ORDERS[p]
        arrive(("z1", p), c_at(p, storage(flipped[z1], y, core), 1), z1)
        arrive(("z2", p), c_at(p, storage(flipped["zz"], y, core), 1), z1)
        y0, y1 = Y_ORDERS[p]
        send(("y0", p), c_at(p, group, 4), c_at(p, group, 4), y0)
        send(("y1", p), c_at(p, group, 4), c_at(p, group, 4), y1)
        send(("c0", p), c_at(p, group, 4), c_at(p, group, 4), "co")
        a, b, c = ORDERS[p]
        arrive(("r0", p), r_at(p, bits[a] * 4 + bits[b] * 2 + 1 - bits[c], 1), c)
        pair = bits[a] * 4 + bits[b] * 2
        send(("r1", p), r_at(p, pair, 2), r_at(p, pair, 2), b)
        if p == 1:
            corner_add(2)
            corner_send(3)
    corner_add(3)
    corner_send(4)

    for p in range(PARTS):
        y0, y1 = Y_ORDERS[p]
        near = storage(0, flipped[y0], core)
        arrive(("y0", p), c_at(p, near, 4), y0)
        send(("y2", p), c_at(p, near, 4), c_at(p, near, 4), y1)
        send(("c1", p), c_at(p, near, 4), c_at(p, near, 4), "co")
        a, b, c = ORDERS[p]
        arrive(("r1", p), r_at(p, bits[a] * 4 + (1 - bits[b]) * 2, 2), b)
        send(("r2", p), r_at(p, bits[a] * 4, 4), r_at(p, bits[a] * 4, 4), a)
        if p == 0:
            corner_add(4)
            ka, kb, kc = CORNER_ORDER
            k0 = bits[ka] * 4 + bits[kb] * 2 + bits[kc]
            k_ref[pl.ds(k0, 1)] = ar[5][None]
            send(("k0",), ar.at[5], k_ref.at[k0], kc)
        if p == 3:
            arrive(("k0",), k_ref.at[bits[ka] * 4 + bits[kb] * 2 + 1 - bits[kc]], kc)
            two = k_ref.at[pl.ds(bits[ka] * 4 + bits[kb] * 2, 2)]
            send(("k1",), two, two, kb)

    for p in range(PARTS):
        y0, y1 = Y_ORDERS[p]
        near = storage(0, flipped[y1], core)
        arrive(("y1", p), c_at(p, near, 4), y1)
        send(("c2", p), c_at(p, near, 4), c_at(p, near, 4), "co")
        if p == 1:
            arrive(("k1",), k_ref.at[pl.ds(bits[ka] * 4 + (1 - bits[kb]) * 2, 2)], kb)
            four = k_ref.at[pl.ds(bits[ka] * 4, 4)]
            send(("k2",), four, four, ka)

    for p in range(PARTS):
        far = storage(0, flipped["yy"], core)
        arrive(("y2", p), c_at(p, far, 4), Y_ORDERS[p][1])
        send(("c3", p), c_at(p, far, 4), c_at(p, far, 4), "co")

    arrive(("k2",), k_ref.at[pl.ds((1 - bits[ka]) * 4, 4)], ka)
    for p in range(PARTS):
        a = ORDERS[p][0]
        arrive(("r2", p), r_at(p, (1 - bits[a]) * 4, 4), a)
        y0, y1 = Y_ORDERS[p]
        arrive(("c0", p), c_at(p, storage(0, y, 1 - core), 4), "co")
        arrive(("c1", p), c_at(p, storage(0, flipped[y0], 1 - core), 4), "co")
        arrive(("c2", p), c_at(p, storage(0, flipped[y1], 1 - core), 4), "co")
        arrive(("c3", p), c_at(p, storage(0, flipped["yy"], 1 - core), 4), "co")

    @pl.when(not_self)
    def _():
        for p in range(PARTS):
            place(p).wait_send()

    for c in sent:
        c.wait_send()


MESSAGES = 3 * PARTS + PARTS + 3 * PARTS + 3 * PARTS + 4 * PARTS + 3 * PARTS + 5 + 3


def live(ids, chosen):
    hit = jnp.max((ids == chosen).astype(F32), axis=1, keepdims=True)
    return 1.0 - hit


def update_kernel(
    pivots_ref, m_ref, w_ref, k_ref, r_ref, c_ref, out_ref, factor_ref, left_hi, left_lo, t_hi, t_lo
):
    j = pl.program_id(0)
    pivots = pivots_ref[...]

    @pl.when(j == 0)
    def _():
        slots = [slot_of(CORNER_ORDER, s) for s in range(8)]
        corner = jnp.concatenate(
            [
                jnp.concatenate(
                    [
                        k_ref[slots[s], (2 * half + h) * EXTRA : (2 * half + h + 1) * EXTRA, :]
                        for h in range(2)
                    ],
                    axis=1,
                )
                for half in range(2)
                for s in range(8)
            ],
            axis=0,
        )
        w_one, w_two = split(w_ref[0]), split(w_ref[1])
        t = split(dot3(w_one, split(corner), NT))
        t_hi[...], t_lo[...] = t
        rows = []
        for p in range(PARTS):
            rows.append(
                jnp.concatenate(
                    [
                        r_ref[p, slot * PIECE : (slot + 1) * PIECE, :]
                        for slot in (slot_of(ORDERS[p], s) for s in range(8))
                    ],
                    axis=0,
                )
            )
        one = jnp.concatenate(rows[:2], axis=1)
        two = jnp.concatenate(rows[2:], axis=1)
        ids = lax.axis_index("row") * ROWS
        ids_one = ids + lax.broadcasted_iota(jnp.int32, (ROWS, NB), 0)
        live_one = live(ids_one, pivots[:, :NB])
        live_two = live_one * live(ids_one, pivots[:, NB:])
        one = split(one)
        factor_one = live_one * dot3(one, w_one, NN)
        two = two - live_one * dot3(one, t, NN)
        factor_two = live_two * dot3(split(two), w_two, NN)
        factor_ref[:, :NB] = factor_one
        factor_ref[:, NB:] = factor_two
        left_hi[:, :NB], left_lo[:, :NB] = split(factor_one)
        left_hi[:, NB:], left_lo[:, NB:] = split(factor_two)

    base = (j // 2) * 16 + (j % 2) * 4

    def piece(p, s):
        slot = base + ((s % 4) // 2) * 8 + (s // 4) * 2 + s % 2
        return c_ref[p, pl.ds(pl.multiple_of(slot * PIECE, 8), PIECE), :]

    def panel(n):
        return jnp.concatenate(
            [
                jnp.concatenate([piece(2 * n, s), piece(2 * n + 1, s)], axis=1)
                for s in range(8)
            ],
            axis=0,
        )

    width = m_ref.shape[1]
    ids = lax.axis_index("col") * COLS + j * width
    ids = ids + lax.broadcasted_iota(jnp.int32, (width, NB), 0)
    live_one = live(ids, pivots[:, :NB])
    live_two = live_one * live(ids, pivots[:, NB:])
    one = live_one * panel(0)
    one_hi, one_lo = split(one)
    two = live_two * (panel(1) - dot3((one_hi, one_lo), (t_hi[...], t_lo[...]), NN))
    two_hi, two_lo = split(two)
    right = (
        jnp.concatenate([one_hi, two_hi], axis=1),
        jnp.concatenate([one_lo, two_lo], axis=1),
    )
    out_ref[...] = m_ref[...] - dot3((left_hi[...], left_lo[...]), right, NT)


def shards(matrix, inverse_blocks, pivots):
    pivots = pivots.reshape(1, NP)
    whole = lambda shape: pl.BlockSpec(
        shape, lambda *_: (0,) * len(shape), pipeline_mode=pl.Buffered(1)
    )
    picked = pl.pallas_call(
        select_kernel,
        name="select",
        grid=(4,),
        out_shape=jax.ShapeDtypeStruct((PARTS, 8 * SLICE, LANES), F32),
        in_specs=[whole((1, NP)), pl.BlockSpec((ROWS, 512), lambda k: (0, k))],
        out_specs=whole((PARTS, 8 * SLICE, LANES)),
        scratch_shapes=[pltpu.VMEM((ROWS, NP), F32)],
    )(pivots, matrix)
    vmem = pl.BlockSpec(memory_space=pltpu.VMEM)
    across, rows, corner = pl.pallas_call(
        exchange_kernel,
        name="exchange",
        out_shape=(
            jax.ShapeDtypeStruct((PARTS, COLS, LANES), F32),
            jax.ShapeDtypeStruct((PARTS, ROWS, LANES), F32),
            jax.ShapeDtypeStruct((8, PARTS * EXTRA, LANES), F32),
        ),
        in_specs=[vmem],
        out_specs=(vmem, vmem, vmem),
        scratch_shapes=[
            pltpu.VMEM((PARTS, 7 * SLICE, LANES), F32),
            pltpu.VMEM((PARTS, 4 * SLICE, LANES), F32),
            pltpu.VMEM((PARTS, 2 * SLICE, LANES), F32),
            pltpu.VMEM((PARTS, SLICE, LANES), F32),
            pltpu.VMEM((6, PARTS * EXTRA, LANES), F32),
            pltpu.VMEM((5, PARTS * EXTRA, LANES), F32),
            pltpu.SemaphoreType.DMA((MESSAGES,)),
            pltpu.SemaphoreType.DMA((MESSAGES,)),
            pltpu.SemaphoreType.DMA((PARTS,)),
        ],
        compiler_params=pltpu.CompilerParams(
            collective_id=0, has_side_effects=True, vmem_limit_bytes=40 << 20
        ),
    )(picked)
    return tuple(
        pl.pallas_call(
            update_kernel,
            name="update",
            grid=(4,),
            out_shape=(
                jax.ShapeDtypeStruct((ROWS, COLS), F32),
                jax.ShapeDtypeStruct((ROWS, NP), F32),
            ),
            in_specs=[
                whole((1, NP)),
                pl.BlockSpec((ROWS, 512), lambda j: (0, j)),
                whole((2, NB, NB)),
                whole((8, PARTS * EXTRA, LANES)),
                whole((PARTS, ROWS, LANES)),
                whole((PARTS, COLS, LANES)),
            ],
            out_specs=(
                pl.BlockSpec((ROWS, 512), lambda j: (0, j)),
                whole((ROWS, NP)),
            ),
            scratch_shapes=[
                pltpu.VMEM((ROWS, NP), BF16),
                pltpu.VMEM((ROWS, NP), BF16),
                pltpu.VMEM((NB, NB), BF16),
                pltpu.VMEM((NB, NB), BF16),
            ],
            compiler_params=pltpu.CompilerParams(vmem_limit_bytes=40 << 20),
        )(pivots, matrix, inverse_blocks, corner, rows, across)
    )


def solution(mesh):
    return jax.shard_map(
        shards,
        mesh=mesh,
        in_specs=(P("row", "col"), P(), P()),
        out_specs=(P("row", "col"), P("row", None)),
        check_vma=False,
    )
```

time: 707 us -> 81.5 us (0.12)
  the two profiles are of different devices: /device:TPU:1 before, /device:TPU:38 now
where the time goes in v1:
time: 81.5 us; the launch traced here: 81.3 us
  Pallas kernels  77.1 us (95%)
  local copies, waits for them, and re-layouts  3.51 us (4%)
    pallas_call x1, Pallas kernels, shards(): pl.pallas_call(exchange_kernel, name='exchange', out_shape=(jax.ShapeDtyp...  61.7 us
    pallas_call x1, Pallas kernels, shards(): pl.pallas_call(update_kernel, name='update', grid=(4,), out_shape=(jax.Sh...  8.88 us
    pallas_call x1, Pallas kernels, shards(): pl.pallas_call(select_kernel, name='select', grid=(4,), out_shape=jax.Sha...  6.58 us
    unnamed x8, local copies, waits for them, and re-layouts  3.51 us

profile of v1, /device:TPU:38, one launch (start us, length us, event | category | flops | bytes accessed | tf_op | source)
XLA Modules:
  0.0 81.3 jit_solution(2028338338706531791)
XLA Ops:
  0.6 0.0 copy-start.3
  0.6 0.0 copy-start.2
  0.6 6.6 %select.1.s_ref = f32[4,640,128]{2,1,0:T(8,128)} custom-call(s32[1,512]{1,0:T(1,128)} %bitcast.1, f32[512,2048]{1,0:T(8,128)} %m_ref.3), custom_call_target="tpu_custom_call" | custom-call | tf_op jit(solution)/shard_map/select/pallas_call | solution.py:445
  7.2 0.0 copy-start.1
  7.2 1.3 %copy-done.1 = f32[4,640,128]{2,1,0:T(8,128)S(1)} copy-done((f32[4,640,128]{2,1,0:T(8,128)S(1)}, f32[4,640,128]{2,1,0:T(8,128)}, u32[]{:S(2)}) %copy-start.1) | copy-done | bytes 1310744
  8.5 61.7 %exchange.1 = (f32[4,2048,128]{2,1,0:T(8,128)S(1)}, f32[4,512,128]{2,1,0:T(8,128)S(1)}, f32[8,64,128]{2,1,0:T(8,128)S(1)}) custom-call(f32[4,640,128]{2,1,0:T(8,128)S(1)} %copy-done.1), custom_call_target="tpu_custom_call" | custom-call | tf_op jit(solution)/shard_map/exchange/pallas_call | solution.py:455
  70.2 0.0 copy-done.3
  70.2 0.0 copy-done.2
  70.2 0.0 copy-start
  70.2 2.2 %copy-done = f32[512,2048]{1,0:T(8,128)S(1)} copy-done((f32[512,2048]{1,0:T(8,128)S(1)}, f32[512,2048]{1,0:T(8,128)}, u32[]{:S(2)}) %copy-start) | copy-done | bytes 4194328
  72.4 8.9 %update.1 = (f32[512,2048]{1,0:T(8,128)}, f32[512,512]{1,0:T(8,128)}) custom-call(s32[1,512]{1,0:T(1,128)S(1)} %bitcast.2, f32[512,2048]{1,0:T(8,128)S(1)} %copy-done, f32[2,256,256]{2,1,0:T(8,128)S(1)} %copy-done.2, f32[8,64,128]{2,1,0:T(8,128)S(1)} %get-tuple-element.5.k_ref, f32[4,512,128]{2,1,0:T(8,128)S(1)} %get-tuple-element.6.r_ref, ...), custom_call_target="tpu_custom_call" | custom-call | tf_op jit(solution)/shard_map/update/pallas_call | solution.py:481
Async XLA Ops:
  0.6 69.6 %copy-start.3 = (s32[512]{0:T(512)S(1)}, s32[512]{0:T(512)}, u32[]{:S(2)}) copy-start(s32[512]{0:T(512)} %param.5) | copy-start | bytes 6148
  0.6 69.6 %copy-start.2 = (f32[2,256,256]{2,1,0:T(8,128)S(1)}, f32[2,256,256]{2,1,0:T(8,128)}, u32[]{:S(2)}) copy-start(f32[2,256,256]{2,1,0:T(8,128)} %w_ref.1) | copy-start | bytes 1572868
  7.2 1.3 %copy-start.1 = (f32[4,640,128]{2,1,0:T(8,128)S(1)}, f32[4,640,128]{2,1,0:T(8,128)}, u32[]{:S(2)}) copy-start(f32[4,640,128]{2,1,0:T(8,128)} %select.1.s_ref) | copy-start | bytes 3932164
  70.2 2.2 %copy-start = (f32[512,2048]{1,0:T(8,128)S(1)}, f32[512,2048]{1,0:T(8,128)}, u32[]{:S(2)}) copy-start(f32[512,2048]{1,0:T(8,128)} %m_ref.3) | copy-start | bytes 12582916

commit v2 on v0

v2 whole, which is shorter than its diff:
```python
import jax
import jax.numpy as jnp
from jax import lax
from jax.experimental import pallas as pl
from jax.experimental.pallas import tpu as pltpu
from jax.sharding import PartitionSpec as P

MESH = pl.DeviceIdType.MESH
F32, BF16 = jnp.float32, jnp.bfloat16
ROWS, COLS, NB, NP = 512, 2048, 256, 512
PARTS, LANES = 4, 128
PIECE = 64
CORNER = PARTS
ORDERS = (
    ("xa", "xb", "zl"),
    ("xb", "xa", "zl"),
    ("xa", "xb", "zl"),
    ("xb", "xa", "zl"),
    ("zl", "xa", "xb"),
)
Z_ORDERS = (("za", "zb"), ("zb", "za"), ("za", "zb"), ("zb", "za"))
Y_ORDERS = (("ya", "yb"), ("yb", "ya"), ("yb", "ya"), ("ya", "yb"))
CORNER_SUM = (("ya", "yb", "yf"), ("za", "zb", "zf"), ("co",))


def flip_a(v):
    return v + 1 - 2 * (v % 2)


def flip_b(v):
    return (v + 2 * (v % 2) + 3) % 4


def bit_a(v):
    return ((v + 1) // 2) % 2


def bit_b(v):
    return v // 2


def target_bits(s):
    x, zl = s % 4, s // 4
    return {"xa": bit_a(x), "xb": bit_b(x), "zl": zl}


def slot_of(order, s):
    b = target_bits(s)
    return b[order[0]] * 4 + b[order[1]] * 2 + b[order[2]]


def split(a):
    hi = a.astype(BF16)
    return hi, (a - hi.astype(F32)).astype(BF16)


def dot(a, b, dims):
    return lax.dot_general(a, b, (dims, ((), ())), preferred_element_type=F32)


def dot3(a, b, dims):
    (ah, al), (bh, bl) = a, b
    return dot(ah, bh, dims) + (dot(ah, bl, dims) + dot(al, bh, dims))


NN = ((1,), (0,))
NT = ((1,), (1,))
TN = ((0,), (0,))


def source_slot(s):
    return (s % 4) * 2 + s // 4


def live(ids, chosen):
    hit = jnp.max((ids == chosen).astype(F32), axis=1, keepdims=True)
    return 1.0 - hit


def panels_kernel(
    pivots_ref,
    w_ref,
    m_hbm,
    out_ref,
    factor_ref,
    m_ref,
    onehot,
    s_ref,
    rx,
    sum_one,
    half,
    q,
    c_ref,
    r_ref,
    k_ref,
    ar,
    arx,
    left_hi,
    left_lo,
    t_hi,
    t_lo,
    send_sem,
    recv_sem,
    own_sem,
    load_sem,
):
    row, col = lax.axis_index("row"), lax.axis_index("col")
    zh, y, core = row // 8, (row % 8) // 2, row % 2
    zl, x = col // 4, col % 4
    bits = {"xa": bit_a(x), "xb": bit_b(x), "zl": zl}

    def device(zh_, y_, core_, zl_, x_):
        return (zh_ * 8 + y_ * 2 + core_, zl_ * 4 + x_)

    def storage(zh_, y_, core_):
        return y_ * 8 + core_ * 4 + zh_

    partner = {
        "xa": device(zh, y, core, zl, flip_a(x)),
        "xb": device(zh, y, core, zl, flip_b(x)),
        "xf": device(zh, y, core, zl, (x + 2) % 4),
        "zl": device(zh, y, core, 1 - zl, x),
        "zf": device((zh + 2) % 4, y, core, zl, x),
        "yf": device(zh, (y + 2) % 4, core, zl, x),
        "za": device(flip_a(zh), y, core, zl, x),
        "zb": device(flip_b(zh), y, core, zl, x),
        "ya": device(zh, flip_a(y), core, zl, x),
        "yb": device(zh, flip_b(y), core, zl, x),
        "co": device(zh, y, 1 - core, zl, x),
    }
    flipped = {
        "za": flip_a(zh),
        "zb": flip_b(zh),
        "ya": flip_a(y),
        "yb": flip_b(y),
        "zz": (zh + 2) % 4,
        "yy": (y + 2) % 4,
    }
    to_x = (zh % 2) * 2 + y // 2
    to_z = (zh + 2 + to_x + 4 - x) % 4
    to_y = y + zl * (flip_b(y) - y)
    dest = device(to_z, to_y, core, zh // 2, to_x)
    dest_slot = storage(to_z, to_y, core)
    from_z = zl * 2 + x // 2
    from_l = (y // 2 + x % 2) % 2
    from_y = y + from_l * (flip_b(y) - y)
    source = device(from_z, from_y, core, from_l, (from_z + 2 + x + 4 - zh) % 4)
    is_self = (dest[0] == row) & (dest[1] == col)
    not_self = jnp.logical_not(is_self)

    HALF = ROWS // 2
    loads = [
        pltpu.make_async_copy(
            m_hbm.at[pl.ds(n * HALF, HALF)], m_ref.at[pl.ds(n * HALF, HALF)], load_sem.at[n]
        )
        for n in range(2)
    ]
    for c in loads:
        c.start()

    barrier = pltpu.get_barrier_semaphore()

    def greet(dev):
        pl.semaphore_signal(barrier, inc=1, device_id=dev, device_id_type=MESH)

    for dev in partner.values():
        greet(dev)

    @pl.when(not_self)
    def _():
        greet(dest)
        greet(source)

    ids = {}
    sent = []

    def copy(key, src, dst, dev):
        n = ids.setdefault(key, len(ids))
        return pltpu.make_async_remote_copy(
            src_ref=src,
            dst_ref=dst,
            send_sem=send_sem.at[n],
            recv_sem=recv_sem.at[n],
            device_id=dev,
            device_id_type=MESH,
        )

    def send(key, src, dst, dim):
        c = copy(key, src, dst, partner[dim])
        c.start()
        sent.append(c)

    def arrive(key, dst, dim):
        copy(key, dst, dst, partner[dim]).wait_recv()

    def at(ref, p, start, size):
        return ref.at[p, pl.ds(pl.multiple_of(start, 8), size), :]

    def load(ref, p, start, size):
        return ref[p, pl.ds(pl.multiple_of(start, 8), size), :]

    PAIR = 2 * PIECE
    across_x = (("xa", flip_a(x)), ("xb", flip_b(x)), ("xf", (x + 2) % 4))

    def rx_at(p, n):
        return rx.at[p, n * PAIR : (n + 1) * PAIR, :]

    def last(p):
        return rx.at[p, 3 * PAIR :, :]

    def scatter_one(p):
        for n, (d, x_) in enumerate(across_x):
            send(("rs0", p, d), at(s_ref, p, x_ * PAIR, PAIR), rx_at(p, n), d)

    def scatter_two(p):
        for n, (d, _) in enumerate(across_x):
            arrive(("rs0", p, d), rx_at(p, n), d)
        near = load(s_ref, p, x * PAIR, PAIR) + rx[p, :PAIR, :]
        far = rx[p, PAIR : 2 * PAIR, :] + rx[p, 2 * PAIR : 3 * PAIR, :]
        sum_one[p] = near + far
        send(("rs1", p), at(sum_one, p, (1 - zl) * PIECE, PIECE), last(p), "zl")

    def scattered(p):
        arrive(("rs1", p), last(p), "zl")
        return load(sum_one, p, zl * PIECE, PIECE) + rx[p, 3 * PAIR :, :]

    def corner_one():
        d = ORDERS[CORNER][0]
        send(("k", 0), at(s_ref, CORNER, (1 - bits[d]) * 256, 256), rx.at[CORNER, :256], d)

    def corner_two():
        d, e = ORDERS[CORNER][:2]
        arrive(("k", 0), rx.at[CORNER, :256], d)
        half[...] = load(s_ref, CORNER, bits[d] * 256, 256) + rx[CORNER, :256]
        start = pl.multiple_of((1 - bits[e]) * 128, 8)
        send(("k", 1), half.at[pl.ds(start, 128)], rx.at[CORNER, 256:384], e)

    def corner_three():
        d, e = ORDERS[CORNER][1:]
        arrive(("k", 1), rx.at[CORNER, 256:384], d)
        kept = half[pl.ds(pl.multiple_of(bits[d] * 128, 8), 128)]
        sum_one[CORNER] = kept + rx[CORNER, 256:384]
        send(("k", 2), at(sum_one, CORNER, (1 - bits[e]) * 64, 64), rx.at[CORNER, 384:448], e)

    mine = storage(zh, y, core)

    def c_at(p, slot, count):
        return at(c_ref, p, slot * PIECE, count * PIECE)

    def place(p):
        return copy(("place", p), q.at[p], c_at(p, dest_slot, 1), dest)

    def keep(p):
        return pltpu.make_async_copy(q.at[p], c_at(p, dest_slot, 1), own_sem.at[p])

    def my_slot(p):
        a, b, c = ORDERS[p]
        return bits[a] * 4 + bits[b] * 2 + bits[c]

    def r_at(p, slot, count):
        return at(r_ref, p, slot * PIECE, count * PIECE)

    def place_part(p):
        q[p] = scattered(p)

        @pl.when(not_self)
        def _():
            place(p).start()

        @pl.when(is_self)
        def _():
            keep(p).start()

        r_ref[p, pl.ds(pl.multiple_of(my_slot(p) * PIECE, 8), PIECE), :] = q[p]
        send(("r0", p), q.at[p], r_at(p, my_slot(p), 1), ORDERS[p][2])

    def row_two(p):
        a, b, c = ORDERS[p]
        arrive(("r0", p), r_at(p, bits[a] * 4 + bits[b] * 2 + 1 - bits[c], 1), c)
        pair = bits[a] * 4 + bits[b] * 2
        send(("r1", p), r_at(p, pair, 2), r_at(p, pair, 2), b)

    def row_three(p):
        a, b, c = ORDERS[p]
        arrive(("r1", p), r_at(p, bits[a] * 4 + (1 - bits[b]) * 2, 2), b)
        send(("r2", p), r_at(p, bits[a] * 4, 4), r_at(p, bits[a] * 4, 4), a)

    def row_done(p):
        a = ORDERS[p][0]
        arrive(("r2", p), r_at(p, (1 - bits[a]) * 4, 4), a)

    def corner_send(n):
        for m, d in enumerate(CORNER_SUM[n]):
            send(("ar", n, d), ar.at[n], arx.at[3 * n + m], d)

    def corner_add(n):
        total = ar[n]
        for m, d in enumerate(CORNER_SUM[n]):
            arrive(("ar", n, d), arx.at[3 * n + m], d)
            total = total + arx[3 * n + m]
        ar[n + 1] = total

    def corner_start():
        d = ORDERS[CORNER][2]
        arrive(("k", 2), rx.at[CORNER, 384:448], d)
        ar[0] = load(sum_one, CORNER, bits[d] * 64, 64) + rx[CORNER, 384:448]
        corner_send(0)

    def corner_step(n):
        corner_add(n - 1)
        corner_send(n)

    def corner_gather(n):
        slot = x * 2 + zl
        if n == 0:
            corner_add(2)
            k_ref[pl.ds(slot, 1)] = ar[3][None]
            send(("g0",), ar.at[3], k_ref.at[slot], "zl")
        if n == 1:
            arrive(("g0",), k_ref.at[x * 2 + 1 - zl], "zl")
            two = k_ref.at[pl.ds(x * 2, 2)]
            for d, _ in across_x:
                send(("g1", d), two, two, d)
        if n == 2:
            for d, x_ in across_x:
                arrive(("g1", d), k_ref.at[pl.ds(x_ * 2, 2)], d)

    def level(p, n):
        z0, z1 = Z_ORDERS[p]
        return (zh, flipped[z0], flipped[z1], flipped["zz"])[n]

    def spread(p, n):
        y0, y1 = Y_ORDERS[p]
        slot = c_at(p, storage(level(p, n), y, core), 1)
        send(("y0", p, n), slot, slot, y0)
        send(("y1", p, n), slot, slot, y1)

    def placed(p):
        @pl.when(not_self)
        def _():
            copy(("place", p), c_at(p, mine, 1), c_at(p, mine, 1), source).wait_recv()

        @pl.when(is_self)
        def _():
            keep(p).wait()

        z0, z1 = Z_ORDERS[p]
        send(("z0", p), c_at(p, mine, 1), c_at(p, mine, 1), z0)
        send(("z1", p), c_at(p, mine, 1), c_at(p, mine, 1), z1)
        spread(p, 0)

    def near_z(p):
        z0, z1 = Z_ORDERS[p]
        slot = c_at(p, storage(level(p, 1), y, core), 1)
        arrive(("z0", p), slot, z0)
        send(("z2", p), slot, slot, z1)
        spread(p, 1)
        arrive(("z1", p), c_at(p, storage(level(p, 2), y, core), 1), z1)
        spread(p, 2)

    def far_z(p):
        z1 = Z_ORDERS[p][1]
        arrive(("z2", p), c_at(p, storage(level(p, 3), y, core), 1), z1)
        spread(p, 3)
        share(p, 0, y)

    def share(p, n, y_):
        block = c_at(p, storage(0, y_, core), 4)
        send(("c", p, n), block, block, "co")

    def near_y(p, n):
        y0, y1 = Y_ORDERS[p]
        slot = c_at(p, storage(level(p, n), flipped[y0], core), 1)
        arrive(("y0", p, n), slot, y0)
        send(("y2", p, n), slot, slot, y1)

    def next_y(p):
        y1 = Y_ORDERS[p][1]
        for n in range(4):
            arrive(("y1", p, n), c_at(p, storage(level(p, n), flipped[y1], core), 1), y1)
        share(p, 2, flipped[y1])

    def far_y(p):
        y1 = Y_ORDERS[p][1]
        for n in range(4):
            arrive(("y2", p, n), c_at(p, storage(level(p, n), flipped["yy"], core), 1), y1)
        share(p, 3, flipped["yy"])

    def shared(p, n):
        y0, y1 = Y_ORDERS[p]
        y_ = (y, flipped[y0], flipped[y1], flipped["yy"])[n]
        arrive(("c", p, n), c_at(p, storage(0, y_, 1 - core), 4), "co")

    pivots = pivots_ref[...]
    row_start, col_start = row * ROWS, col * COLS

    def choose(h):
        places = lax.broadcasted_iota(jnp.int32, (COLS, NB), 0) + col_start
        onehot[...] = (places == pivots[:, h * NB : (h + 1) * NB]).astype(F32).astype(BF16)
        corner = None
        for n in range(2):
            if h == 0:
                loads[n].wait()
            hi, lo = split(m_ref[n * HALF : (n + 1) * HALF, :])
            picked = dot(hi, onehot[...], NN) + dot(lo, onehot[...], NN)
            for g in range(2):
                p = 2 * h + g
                for s in range(4 * n, 4 * n + 4):
                    slot = source_slot(s) * PIECE
                    s_ref[p, slot : slot + PIECE, :] = picked[
                        s * PIECE - n * HALF : (s + 1) * PIECE - n * HALF,
                        g * LANES : (g + 1) * LANES,
                    ]
            if h == 0:
                places = lax.broadcasted_iota(jnp.int32, (HALF, NB), 0) + (row_start + n * HALF)
                chosen = (places == pivots[:, NB:]).astype(F32).astype(BF16)
                hi, lo = split(picked)
                term = dot(chosen, hi, TN) + dot(chosen, lo, TN)
                corner = term if corner is None else corner + term
        return corner

    corner = choose(0)

    @pl.when(not_self)
    def _():
        pl.semaphore_wait(barrier, len(partner) + 2)

    @pl.when(is_self)
    def _():
        pl.semaphore_wait(barrier, len(partner))

    scatter_one(0)
    for s in range(8):
        slot = slot_of(ORDERS[CORNER], s) * PIECE
        for g in range(2):
            s_ref[CORNER, slot + g * 32 : slot + (g + 1) * 32, :] = corner[
                s * 32 : (s + 1) * 32, g * LANES : (g + 1) * LANES
            ]
    corner_one()
    scatter_one(1)
    choose(1)
    corner_two()
    scatter_one(2)
    scatter_two(0)
    corner_three()
    scatter_one(3)
    place_part(0)
    scatter_two(1)
    corner_start()
    place_part(1)
    placed(0)
    scatter_two(2)
    corner_step(1)
    near_z(0)
    place_part(2)
    near_y(0, 0)
    placed(1)
    scatter_two(3)
    near_y(0, 1)
    near_y(0, 2)
    far_z(0)
    near_z(1)
    place_part(3)
    placed(2)
    near_y(1, 0)
    corner_step(2)
    row_two(0)
    row_two(1)
    near_y(0, 3)
    share(0, 1, flipped[Y_ORDERS[0][0]])
    near_y(1, 1)
    near_y(1, 2)
    far_z(1)
    near_z(2)
    corner_gather(0)
    placed(3)
    near_y(2, 0)
    row_two(2)
    row_two(3)
    corner_gather(1)
    near_y(1, 3)
    share(1, 1, flipped[Y_ORDERS[1][0]])
    far_z(2)
    near_z(3)
    near_y(2, 1)
    near_y(2, 2)
    row_three(0)
    row_three(1)
    near_y(3, 0)
    far_z(3)
    near_y(2, 3)
    share(2, 1, flipped[Y_ORDERS[2][0]])
    row_three(2)
    row_three(3)
    near_y(3, 1)
    near_y(3, 2)
    near_y(3, 3)
    share(3, 1, flipped[Y_ORDERS[3][0]])
    corner_gather(2)
    for p in range(PARTS):
        row_done(p)

    slots = [source_slot(s) for s in range(8)]
    corner = jnp.concatenate(
        [
            jnp.concatenate([k_ref[slot, :32, :], k_ref[slot, 32:, :]], axis=1)
            for slot in slots
        ],
        axis=0,
    )
    w_one, w_two = split(w_ref[0]), split(w_ref[1])
    t = split(dot3(w_one, split(corner), NT))
    t_hi[...], t_lo[...] = t
    rows = [
        jnp.concatenate(
            [
                r_ref[p, slot * PIECE : (slot + 1) * PIECE, :]
                for slot in (slot_of(ORDERS[p], s) for s in range(8))
            ],
            axis=0,
        )
        for p in range(PARTS)
    ]
    row_ids = row_start + lax.broadcasted_iota(jnp.int32, (ROWS, NB), 0)
    live_one = live(row_ids, pivots[:, :NB])
    live_two = live_one * live(row_ids, pivots[:, NB:])
    one = split(jnp.concatenate(rows[:2], axis=1))
    factor_one = live_one * dot3(one, w_one, NN)
    two = jnp.concatenate(rows[2:], axis=1) - live_one * dot3(one, t, NN)
    factor_two = live_two * dot3(split(two), w_two, NN)
    factor_ref[:, :NB] = factor_one
    factor_ref[:, NB:] = factor_two
    left_hi[:, :NB], left_lo[:, :NB] = split(factor_one)
    left_hi[:, NB:], left_lo[:, NB:] = split(factor_two)

    def update(y_, core_):
        over = (y_ // 2 + x % 2) % 2
        y_from = y_ + over * (flip_b(y_) - y_)
        start = ((y_from % 2) * 2 + core_) * 512 + over * 256
        first = [
            storage((from_z + 2 + x + 4 - s) % 4, y_, core_) * PIECE for s in range(4)
        ]
        piece = [
            jnp.concatenate([load(c_ref, p, f, PIECE) for f in first], axis=0)
            for p in range(PARTS)
        ]
        place_ = lax.broadcasted_iota(jnp.int32, (4 * PIECE, NB), 0)
        place_ = place_ + (col_start + start)
        live_one = live(place_, pivots[:, :NB])
        live_two = live_one * live(place_, pivots[:, NB:])
        one = live_one * jnp.concatenate(piece[:2], axis=1)
        one_hi, one_lo = split(one)
        two = jnp.concatenate(piece[2:], axis=1)
        two = live_two * (two - dot3((one_hi, one_lo), (t_hi[...], t_lo[...]), NN))
        two_hi, two_lo = split(two)
        right = (
            jnp.concatenate([one_hi, two_hi], axis=1),
            jnp.concatenate([one_lo, two_lo], axis=1),
        )
        term = dot3((left_hi[...], left_lo[...]), right, NT)
        columns = pl.ds(pl.multiple_of(start, NB), NB)
        out_ref[:, columns] = m_ref[:, columns] - term

    for p in range(PARTS):
        next_y(p)
    update(y, core)
    for p in range(PARTS):
        shared(p, 0)
    update(y, 1 - core)
    update(flipped["ya"], core)
    for p in range(PARTS):
        far_y(p)
    update(flipped["yb"], core)
    for p in range(PARTS):
        shared(p, 1)
        shared(p, 2)
    update(flipped["ya"], 1 - core)
    update(flipped["yb"], 1 - core)
    update(flipped["yy"], core)
    for p in range(PARTS):
        shared(p, 3)
    update(flipped["yy"], 1 - core)

    @pl.when(not_self)
    def _():
        for p in range(PARTS):
            place(p).wait_send()

    for c in sent:
        c.wait_send()
    assert len(ids) == MESSAGES, len(ids)


MESSAGES = (4 + 1 + 3 + 12 + 4 + 3) * PARTS + 3 + 7 + 4


def shards(matrix, inverse_blocks, pivots):
    vmem = pl.BlockSpec(memory_space=pltpu.VMEM)

    def panel(rows):
        return pltpu.VMEM((PARTS + 1, rows, LANES), F32)

    return tuple(
        pl.pallas_call(
            panels_kernel,
            name="panels",
            out_shape=(
                jax.ShapeDtypeStruct((ROWS, COLS), F32),
                jax.ShapeDtypeStruct((ROWS, NP), F32),
            ),
            in_specs=[vmem, vmem, pl.BlockSpec(memory_space=pltpu.HBM)],
            out_specs=(vmem, vmem),
            scratch_shapes=[
                pltpu.VMEM((ROWS, COLS), F32),
                pltpu.VMEM((COLS, NB), BF16),
                panel(8 * PIECE),
                panel(7 * PIECE),
                panel(2 * PIECE),
                pltpu.VMEM((4 * PIECE, LANES), F32),
                pltpu.VMEM((PARTS, PIECE, LANES), F32),
                pltpu.VMEM((PARTS, COLS, LANES), F32),
                pltpu.VMEM((PARTS, ROWS, LANES), F32),
                pltpu.VMEM((8, PIECE, LANES), F32),
                pltpu.VMEM((4, PIECE, LANES), F32),
                pltpu.VMEM((7, PIECE, LANES), F32),
                pltpu.VMEM((ROWS, NP), BF16),
                pltpu.VMEM((ROWS, NP), BF16),
                pltpu.VMEM((NB, NB), BF16),
                pltpu.VMEM((NB, NB), BF16),
                pltpu.SemaphoreType.DMA((MESSAGES,)),
                pltpu.SemaphoreType.DMA((MESSAGES,)),
                pltpu.SemaphoreType.DMA((PARTS,)),
                pltpu.SemaphoreType.DMA((2,)),
            ],
            compiler_params=pltpu.CompilerParams(
                collective_id=0, has_side_effects=True, vmem_limit_bytes=48 << 20
            ),
        )(pivots.reshape(1, NP), inverse_blocks, matrix)
    )


def solution(mesh):
    return jax.shard_map(
        shards,
        mesh=mesh,
        in_specs=(P("row", "col"), P(), P()),
        out_specs=(P("row", "col"), P("row", None)),
        check_vma=False,
    )
```

time: 707 us -> 74.3 us (0.11)
  waiting for transfers between devices: 628 us -> 0 us
  Pallas kernels: 0 us -> 68.8 us
  matrix products: 26.7 us -> 0 us
  local copies, waits for them, and re-layouts: 30.9 us -> 4.7 us
  between operations: 14 us -> 0.65 us
    psum x3 -> x0, waiting for transfers between devices: 628 us -> none  [the longest x1 302 us: shards(): across = lax.psum(slots, 'row').reshape(pivots.shape[0], tile_cols)]
    pallas_call x0 -> x1, Pallas kernels: none -> 68.8 us  [shards(): pl.pallas_call(panels_kernel, name='panels', out_shape=(jax.ShapeDtypeStr...]
    dot_general x7 -> x0, matrix products: 26.7 us -> none  [product(): jnp.dot(left, right, precision=lax.Precision.HIGHEST, preferred_element_t...]
    gather x4 -> x0, local copies, waits for them, and re-layouts: 10.1 us -> none  [the longest x3 5.51 us: select_columns(): jnp.take(source, jnp.clip(local_idx, 0, source.shape[1] - 1), axis=1)]
  transfers between devices with their start and end apart: 3 -> 0, of which waited for: 3 -> 0; matrix products, arithmetic and copies ran while one was open for 3% -> 0% of each run, Pallas kernels for 0% -> 0%
where the time goes in v2:
time: 74.3 us; the launch traced here: 74.2 us
  Pallas kernels  68.8 us (93%)
  local copies, waits for them, and re-layouts  4.7 us (6%)
    pallas_call x1, Pallas kernels, shards(): pl.pallas_call(panels_kernel, name='panels', out_shape=(jax.ShapeDtypeStr...  68.8 us
    unnamed x6, local copies, waits for them, and re-layouts  4.7 us

profile of v2, /device:TPU:1, one launch (start us, length us, event | category | flops | bytes accessed | tf_op | source)
XLA Modules:
  0.0 74.2 jit_solution(3486257855379771907)
XLA Ops:
  0.6 0.0 copy-start
  0.6 1.0 %copy-done = f32[2,256,256]{2,1,0:T(8,128)S(1)} copy-done((f32[2,256,256]{2,1,0:T(8,128)S(1)}, f32[2,256,256]{2,1,0:T(8,128)}, u32[]{:S(2)}) %copy-start) | copy-done | bytes 524312
  1.7 0.0 copy-start.1
  1.7 0.7 copy-done.1
  2.4 68.8 %panels.1 = (f32[512,2048]{1,0:T(8,128)S(1)}, f32[512,512]{1,0:T(8,128)S(1)}) custom-call(s32[1,512]{1,0:T(1,128)S(1)} %bitcast.1, f32[2,256,256]{2,1,0:T(8,128)S(1)} %copy-done, f32[512,2048]{1,0:T(8,128)} %m_hbm.1), custom_call_target="tpu_custom_call" | custom-call | tf_op jit(solution)/shard_map/panels/pallas_call | solution.py:604
  71.2 2.0 %copy.7 = f32[512,2048]{1,0:T(8,128)} copy(f32[512,2048]{1,0:T(8,128)S(1)} %get-tuple-element.4) | data formatting | bytes 8388608
  73.2 1.0 %copy.8 = f32[512,512]{1,0:T(8,128)} copy(f32[512,512]{1,0:T(8,128)S(1)} %get-tuple-element.5) | data formatting | bytes 2097152
Async XLA Ops:
  0.6 1.0 %copy-start = (f32[2,256,256]{2,1,0:T(8,128)S(1)}, f32[2,256,256]{2,1,0:T(8,128)}, u32[]{:S(2)}) copy-start(f32[2,256,256]{2,1,0:T(8,128)} %w_ref.1) | copy-start | bytes 1572868
  1.7 0.7 copy-start.1
